TPU v7x, 128 devices: a whole 4x4x4 slice. The times are simulated.
128 devices in a mesh: rows: 16 (over x, z), cols: 8 (over y, core).
Axes of the slice: x: 4, y: 4, z: 4, core: 2. Of those that a mesh axis runs over, the one named last changes fastest.
Arguments:
- panel_cols: bfloat16 [64, 32, 256, 128], P('rows', 'cols'), may hold values from -1.75 to 1.75
- pivot_inv: bfloat16 [32, 256, 256], P('cols'), may hold values from -0.375 to 0.375
- pivot_rows: bfloat16 [32, 48, 256, 128], P('rows', 'cols'), may hold values from -1.75 to 1.75
- target_factors: bfloat16 [64, 48, 256, 128], P('rows', 'cols'), may hold values from -5 to 5
- near_blocks: bfloat16 [64, 8, 256, 256], P('rows', 'cols'), may hold values from -6 to 6
- near_cols: int32 [64, 8], P('rows', 'cols'), may hold values from 0 to 5, as said below
- sketch: bfloat16 [48, 256, 64], P('cols'), may hold values from -6 to 6
Outputs:
- near_out: bfloat16 [64, 8, 256, 256], P('rows', 'cols')
- far_out: bfloat16 [64, 48, 256, 128], P('rows', 'cols')
Inputs may be any that keep to these rules, and one draw needn't show every extreme that they name: `near_cols`: for every block row, the 1 entries of each group of slots s with equal s // 1 are distinct.
All inputs are finite; a program needn't handle non-finite values.
Results may differ from a plain program's by a relative error of at most 0.009.
Values may be sent and summed in bfloat16 or wider, within the bound.
A program may use at most 128 MiB of HBM per device.

v0:
```python
import math
import jax
import jax.numpy as jnp
from jax import lax
from jax.sharding import PartitionSpec as P


def spread(block, axis, holder):
    block = jnp.where(lax.axis_index(axis) == holder, block, jnp.zeros_like(block))
    return lax.psum(block, axis)


def product_of(form, left, right):
    return jnp.einsum(form, left, right, preferred_element_type=jnp.float32)


def row_update(left_row, rows_all, target_row, near_row, near_index, sketch):
    half = left_row.shape[-1] // 2
    root_size = math.sqrt(left_row.shape[1])
    left_x = left_row[..., :half]
    left_y = left_row[..., half:]
    pivot_p = rows_all[..., :half]
    pivot_q = rows_all[..., half:]
    mid_cores = product_of("kbr,kjbs->kjrs", left_y, pivot_p).astype(jnp.bfloat16)
    left_terms = product_of("kbr,kjrs->jkbs", left_x, mid_cores).astype(jnp.bfloat16)
    left_near = jnp.take(left_terms, near_index, axis=0)
    q_near = jnp.take(pivot_q, near_index, axis=1)
    update = product_of("nkbs,kncs->nbc", left_near, q_near)
    near_new = (near_row.astype(jnp.float32) - update).astype(jnp.bfloat16)
    column_ids = jnp.arange(target_row.shape[0], dtype=jnp.int32)
    is_near = jnp.any(near_index[:, None] == column_ids[None, :], axis=0)
    target_u = target_row[..., :half]
    target_v = target_row[..., half:]
    sketch_core = product_of("jbs,jbt->jst", target_v, sketch).astype(jnp.bfloat16)
    pivot_sketch = product_of("kjbs,jbt->jkst", pivot_q, sketch).astype(jnp.bfloat16)
    sampled = product_of("jbs,jst->jbt", target_u, sketch_core) - product_of(
        "jkbs,jkst->jbt", left_terms, pivot_sketch
    )
    gram_matrix = jnp.einsum("jbs,jbt->jst", sampled, sampled, precision=lax.Precision.HIGHEST)
    factor_chol = jnp.linalg.cholesky(gram_matrix)
    orthonormal = lax.linalg.triangular_solve(
        factor_chol, sampled, left_side=False, lower=True, transpose_a=True
    )
    basis = (root_size * orthonormal).astype(jnp.bfloat16)
    basis_core = product_of("jbs,jbt->jst", target_u, basis).astype(jnp.bfloat16)
    left_core = product_of("jkbs,jbt->jkst", left_terms, basis).astype(jnp.bfloat16)
    weights_out = (
        product_of("jbs,jst->jbt", target_v, basis_core)
        - product_of("kjbs,jkst->jbt", pivot_q, left_core)
    ) / root_size
    keep_far = jnp.where(is_near, 0.0, 1.0).astype(jnp.bfloat16)[:, None, None]
    far_new = jnp.concatenate([basis, weights_out.astype(jnp.bfloat16)], axis=-1) * keep_far
    return (near_new, far_new)


def per_device(panel_cols, pivot_inv, pivot_rows, target_factors, near_blocks, near_cols, sketch):
    half = panel_cols.shape[-1] // 2
    col_left = panel_cols[..., :half]
    col_right = panel_cols[..., half:]
    pivot_right = product_of("kab,ikar->ikbr", pivot_inv, col_right).astype(jnp.bfloat16)
    local_panel = jnp.concatenate([col_left, pivot_right], axis=-1)
    panel_all = lax.all_gather(local_panel, "cols", axis=1, tiled=True)
    owned = pivot_rows.shape[0]
    row_count = lax.axis_size("rows")

    def fetch(owner, buffer):
        arrived = spread(pivot_rows, "rows", owner)
        return lax.dynamic_update_slice_in_dim(
            buffer, arrived, (owner * owned).astype(jnp.int32), 0
        )

    empty = jnp.zeros((row_count * owned,) + pivot_rows.shape[1:], jnp.bfloat16)
    rows_all = lax.fori_loop(0, row_count, fetch, empty)

    def one_row(row_items):
        return row_update(row_items[0], rows_all, row_items[1], row_items[2], row_items[3], sketch)

    near_new, far_new = lax.map(one_row, (panel_all, target_factors, near_blocks, near_cols))
    return (near_new, far_new)


def solution(mesh):
    placed = (
        P("rows", "cols", None, None),
        P("cols", None, None),
        P("rows", "cols", None, None),
        P("rows", "cols", None, None),
        P("rows", "cols", None, None),
        P("rows", "cols"),
        P("cols", None, None),
    )
    return jax.shard_map(
        per_device,
        mesh=mesh,
        in_specs=placed,
        out_specs=(P("rows", "cols", None, None), P("rows", "cols", None, None)),
        check_vma=False,
    )
```

profile of v0, /device:TPU:1, one launch (start us, length us, event | category | flops | bytes accessed | tf_op | source)
XLA Modules:
  0.0 2002.7 jit_solution(16693872794983531070)
XLA Ops:
  20.1 1473.8 %while.29 = (s32[]{:T(128)}, bf16[32,6,256,128]{3,2,1,0:T(8,128)(2,1)}, bf16[2,6,256,128]{3,2,1,0:T(8,128)(2,1)S(1)}, s32[]{:T(128)}, u32[]{:T(128)}, /*index=5*/u32[]{:T(128)}, s32[]{:T(128)}, s32[]{:T(128)}, s32[]{:T(128)}) while((s32[]{:T(128)}, bf16[32,6,256,128]{3,2,1,0:T(8,128)(2,1)}, bf16[2,6,256,128]{3,2,1,0:T(8,128)(2,1)S(1)}, ...), condition=%wide.region_2.3_spmd, body=%wide.region_0.2_spmd.sunk | while | flops 786442 | bytes 7864545 | solution.py:73
  21.1 91.7 %all-reduce.2.cloned.1.call-done = bf16[2,6,256,128]{3,2,1,0:T(8,128)(2,1)} async-done(((bf16[2,6,256,128]{3,2,1,0:T(8,128)(2,1)}), bf16[2,6,256,128]{3,2,1,0:T(8,128)(2,1)}) %all-reduce.2.cloned.1.call-update) | async-done | bytes 786448 | tf_op jit(solution)/shard_map/while/body/eval_jaxpr/psum | solution.py:10
  115.9 89.1 %all-reduce.2.cloned.1.call-done = bf16[2,6,256,128]{3,2,1,0:T(8,128)(2,1)} async-done(((bf16[2,6,256,128]{3,2,1,0:T(8,128)(2,1)}), bf16[2,6,256,128]{3,2,1,0:T(8,128)(2,1)}) %all-reduce.2.cloned.1.call-update) | async-done | bytes 786448 | tf_op jit(solution)/shard_map/while/body/eval_jaxpr/psum | solution.py:10
  207.9 89.1 %all-reduce.2.cloned.1.call-done = bf16[2,6,256,128]{3,2,1,0:T(8,128)(2,1)} async-done(((bf16[2,6,256,128]{3,2,1,0:T(8,128)(2,1)}), bf16[2,6,256,128]{3,2,1,0:T(8,128)(2,1)}) %all-reduce.2.cloned.1.call-update) | async-done | bytes 786448 | tf_op jit(solution)/shard_map/while/body/eval_jaxpr/psum | solution.py:10
  300.0 88.7 %all-reduce.2.cloned.1.call-done = bf16[2,6,256,128]{3,2,1,0:T(8,128)(2,1)} async-done(((bf16[2,6,256,128]{3,2,1,0:T(8,128)(2,1)}), bf16[2,6,256,128]{3,2,1,0:T(8,128)(2,1)}) %all-reduce.2.cloned.1.call-update) | async-done | bytes 786448 | tf_op jit(solution)/shard_map/while/body/eval_jaxpr/psum | solution.py:10
  391.8 88.7 %all-reduce.2.cloned.1.call-done = bf16[2,6,256,128]{3,2,1,0:T(8,128)(2,1)} async-done(((bf16[2,6,256,128]{3,2,1,0:T(8,128)(2,1)}), bf16[2,6,256,128]{3,2,1,0:T(8,128)(2,1)}) %all-reduce.2.cloned.1.call-update) | async-done | bytes 786448 | tf_op jit(solution)/shard_map/while/body/eval_jaxpr/psum | solution.py:10
  483.6 88.7 %all-reduce.2.cloned.1.call-done = bf16[2,6,256,128]{3,2,1,0:T(8,128)(2,1)} async-done(((bf16[2,6,256,128]{3,2,1,0:T(8,128)(2,1)}), bf16[2,6,256,128]{3,2,1,0:T(8,128)(2,1)}) %all-reduce.2.cloned.1.call-update) | async-done | bytes 786448 | tf_op jit(solution)/shard_map/while/body/eval_jaxpr/psum | solution.py:10
  575.4 89.1 %all-reduce.2.cloned.1.call-done = bf16[2,6,256,128]{3,2,1,0:T(8,128)(2,1)} async-done(((bf16[2,6,256,128]{3,2,1,0:T(8,128)(2,1)}), bf16[2,6,256,128]{3,2,1,0:T(8,128)(2,1)}) %all-reduce.2.cloned.1.call-update) | async-done | bytes 786448 | tf_op jit(solution)/shard_map/while/body/eval_jaxpr/psum | solution.py:10
  667.5 89.1 %all-reduce.2.cloned.1.call-done = bf16[2,6,256,128]{3,2,1,0:T(8,128)(2,1)} async-done(((bf16[2,6,256,128]{3,2,1,0:T(8,128)(2,1)}), bf16[2,6,256,128]{3,2,1,0:T(8,128)(2,1)}) %all-reduce.2.cloned.1.call-update) | async-done | bytes 786448 | tf_op jit(solution)/shard_map/while/body/eval_jaxpr/psum | solution.py:10
  759.6 89.1 %all-reduce.2.cloned.1.call-done = bf16[2,6,256,128]{3,2,1,0:T(8,128)(2,1)} async-done(((bf16[2,6,256,128]{3,2,1,0:T(8,128)(2,1)}), bf16[2,6,256,128]{3,2,1,0:T(8,128)(2,1)}) %all-reduce.2.cloned.1.call-update) | async-done | bytes 786448 | tf_op jit(solution)/shard_map/while/body/eval_jaxpr/psum | solution.py:10
  851.7 88.7 %all-reduce.2.cloned.1.call-done = bf16[2,6,256,128]{3,2,1,0:T(8,128)(2,1)} async-done(((bf16[2,6,256,128]{3,2,1,0:T(8,128)(2,1)}), bf16[2,6,256,128]{3,2,1,0:T(8,128)(2,1)}) %all-reduce.2.cloned.1.call-update) | async-done | bytes 786448 | tf_op jit(solution)/shard_map/while/body/eval_jaxpr/psum | solution.py:10
  943.5 89.1 %all-reduce.2.cloned.1.call-done = bf16[2,6,256,128]{3,2,1,0:T(8,128)(2,1)} async-done(((bf16[2,6,256,128]{3,2,1,0:T(8,128)(2,1)}), bf16[2,6,256,128]{3,2,1,0:T(8,128)(2,1)}) %all-reduce.2.cloned.1.call-update) | async-done | bytes 786448 | tf_op jit(solution)/shard_map/while/body/eval_jaxpr/psum | solution.py:10
  1035.6 88.7 %all-reduce.2.cloned.1.call-done = bf16[2,6,256,128]{3,2,1,0:T(8,128)(2,1)} async-done(((bf16[2,6,256,128]{3,2,1,0:T(8,128)(2,1)}), bf16[2,6,256,128]{3,2,1,0:T(8,128)(2,1)}) %all-reduce.2.cloned.1.call-update) | async-done | bytes 786448 | tf_op jit(solution)/shard_map/while/body/eval_jaxpr/psum | solution.py:10
  1127.4 89.1 %all-reduce.2.cloned.1.call-done = bf16[2,6,256,128]{3,2,1,0:T(8,128)(2,1)} async-done(((bf16[2,6,256,128]{3,2,1,0:T(8,128)(2,1)}), bf16[2,6,256,128]{3,2,1,0:T(8,128)(2,1)}) %all-reduce.2.cloned.1.call-update) | async-done | bytes 786448 | tf_op jit(solution)/shard_map/while/body/eval_jaxpr/psum | solution.py:10
  1219.5 88.7 %all-reduce.2.cloned.1.call-done = bf16[2,6,256,128]{3,2,1,0:T(8,128)(2,1)} async-done(((bf16[2,6,256,128]{3,2,1,0:T(8,128)(2,1)}), bf16[2,6,256,128]{3,2,1,0:T(8,128)(2,1)}) %all-reduce.2.cloned.1.call-update) | async-done | bytes 786448 | tf_op jit(solution)/shard_map/while/body/eval_jaxpr/psum | solution.py:10
  1311.3 88.7 %all-reduce.2.cloned.1.call-done = bf16[2,6,256,128]{3,2,1,0:T(8,128)(2,1)} async-done(((bf16[2,6,256,128]{3,2,1,0:T(8,128)(2,1)}), bf16[2,6,256,128]{3,2,1,0:T(8,128)(2,1)}) %all-reduce.2.cloned.1.call-update) | async-done | bytes 786448 | tf_op jit(solution)/shard_map/while/body/eval_jaxpr/psum | solution.py:10
  1403.1 88.7 %all-reduce.2.cloned.1.call-done = bf16[2,6,256,128]{3,2,1,0:T(8,128)(2,1)} async-done(((bf16[2,6,256,128]{3,2,1,0:T(8,128)(2,1)}), bf16[2,6,256,128]{3,2,1,0:T(8,128)(2,1)}) %all-reduce.2.cloned.1.call-update) | async-done | bytes 786448 | tf_op jit(solution)/shard_map/while/body/eval_jaxpr/psum | solution.py:10
  1494.5 16.8 copy.60
  1511.4 16.6 copy.62
  1546.7 447.8 %while.30 = (s32[]{:T(128)}, bf16[4,1,256,256]{3,2,1,0:T(8,128)(2,1)}, bf16[4,6,256,128]{3,2,1,0:T(8,128)(2,1)}, bf16[4,1,256,256]{3,2,1,0:T(8,128)(2,1)}, s32[4...) while((s32[]{:T(128)}, ...), condition=%wide.region_6.7_spmd, body=%wide.region_3.6_spmd.sunk | while | flops 2490991104 | bytes 93083896 | solution.py:78
  1553.2 10.2 convolution_convert_fusion.5
  1571.4 35.2 %custom-call.15 = f32[6,64,64]{2,1,0:T(8,128)S(1)} custom-call(f32[6,64,64]{2,1,0:T(8,128)S(1)} %fusion.126), custom_call_target="Cholesky" | custom-call | tf_op jit(solution)/shard_map/while/body/eval_jaxpr/jit(cholesky)/cholesky | solution.py:40
  1606.9 29.5 %custom-call.16 = f32[6,1,64,64]{2,3,1,0:T(8,128)S(1)} custom-call(f32[6,1,64,64]{3,2,1,0:T(8,128)S(1)} %select_bitcast_fusion.2), custom_call_target="InvertDiagBlocksLowerTriangular" | custom-call | tf_op jit(solution)/shard_map/while/body/eval_jaxpr/triangular_solve | solution.py:41
  1665.1 10.2 convolution_convert_fusion.5
  1683.4 35.2 %custom-call.15 = f32[6,64,64]{2,1,0:T(8,128)S(1)} custom-call(f32[6,64,64]{2,1,0:T(8,128)S(1)} %fusion.126), custom_call_target="Cholesky" | custom-call | tf_op jit(solution)/shard_map/while/body/eval_jaxpr/jit(cholesky)/cholesky | solution.py:40
  1718.8 29.5 %custom-call.16 = f32[6,1,64,64]{2,3,1,0:T(8,128)S(1)} custom-call(f32[6,1,64,64]{3,2,1,0:T(8,128)S(1)} %select_bitcast_fusion.2), custom_call_target="InvertDiagBlocksLowerTriangular" | custom-call | tf_op jit(solution)/shard_map/while/body/eval_jaxpr/triangular_solve | solution.py:41
  1777.1 10.2 convolution_convert_fusion.5
  1795.3 35.2 %custom-call.15 = f32[6,64,64]{2,1,0:T(8,128)S(1)} custom-call(f32[6,64,64]{2,1,0:T(8,128)S(1)} %fusion.126), custom_call_target="Cholesky" | custom-call | tf_op jit(solution)/shard_map/while/body/eval_jaxpr/jit(cholesky)/cholesky | solution.py:40
  1830.8 29.5 %custom-call.16 = f32[6,1,64,64]{2,3,1,0:T(8,128)S(1)} custom-call(f32[6,1,64,64]{3,2,1,0:T(8,128)S(1)} %select_bitcast_fusion.2), custom_call_target="InvertDiagBlocksLowerTriangular" | custom-call | tf_op jit(solution)/shard_map/while/body/eval_jaxpr/triangular_solve | solution.py:41
  1889.1 10.2 convolution_convert_fusion.5
  1907.3 35.2 %custom-call.15 = f32[6,64,64]{2,1,0:T(8,128)S(1)} custom-call(f32[6,64,64]{2,1,0:T(8,128)S(1)} %fusion.126), custom_call_target="Cholesky" | custom-call | tf_op jit(solution)/shard_map/while/body/eval_jaxpr/jit(cholesky)/cholesky | solution.py:40
  1942.8 29.5 %custom-call.16 = f32[6,1,64,64]{2,3,1,0:T(8,128)S(1)} custom-call(f32[6,1,64,64]{3,2,1,0:T(8,128)S(1)} %select_bitcast_fusion.2), custom_call_target="InvertDiagBlocksLowerTriangular" | custom-call | tf_op jit(solution)/shard_map/while/body/eval_jaxpr/triangular_solve | solution.py:41
  (185 shorter events, 222.1 us)
Async XLA Ops:
  8.0 2.4 copy-start
  12.3 7.8 copy-start.2
  20.1 92.7 %all-reduce.2.cloned.1.call-start = ((), (), s32[]{:S(2)}) async-start(), calls=%async_computation.1 | async-start | bytes 1572864 | tf_op jit(solution)/shard_map/while/body/eval_jaxpr/psum | solution.py:10
  114.9 90.0 %all-reduce.2.cloned.1.call-start = ((), (), s32[]{:S(2)}) async-start(), calls=%async_computation.1 | async-start | bytes 1572864 | tf_op jit(solution)/shard_map/while/body/eval_jaxpr/psum | solution.py:10
  207.0 90.0 %all-reduce.2.cloned.1.call-start = ((), (), s32[]{:S(2)}) async-start(), calls=%async_computation.1 | async-start | bytes 1572864 | tf_op jit(solution)/shard_map/while/body/eval_jaxpr/psum | solution.py:10
  299.1 89.7 %all-reduce.2.cloned.1.call-start = ((), (), s32[]{:S(2)}) async-start(), calls=%async_computation.1 | async-start | bytes 1572864 | tf_op jit(solution)/shard_map/while/body/eval_jaxpr/psum | solution.py:10
  390.9 89.7 %all-reduce.2.cloned.1.call-start = ((), (), s32[]{:S(2)}) async-start(), calls=%async_computation.1 | async-start | bytes 1572864 | tf_op jit(solution)/shard_map/while/body/eval_jaxpr/psum | solution.py:10
  482.6 89.7 %all-reduce.2.cloned.1.call-start = ((), (), s32[]{:S(2)}) async-start(), calls=%async_computation.1 | async-start | bytes 1572864 | tf_op jit(solution)/shard_map/while/body/eval_jaxpr/psum | solution.py:10
  574.4 90.0 %all-reduce.2.cloned.1.call-start = ((), (), s32[]{:S(2)}) async-start(), calls=%async_computation.1 | async-start | bytes 1572864 | tf_op jit(solution)/shard_map/while/body/eval_jaxpr/psum | solution.py:10
  666.5 90.0 %all-reduce.2.cloned.1.call-start = ((), (), s32[]{:S(2)}) async-start(), calls=%async_computation.1 | async-start | bytes 1572864 | tf_op jit(solution)/shard_map/while/body/eval_jaxpr/psum | solution.py:10
  758.6 90.0 %all-reduce.2.cloned.1.call-start = ((), (), s32[]{:S(2)}) async-start(), calls=%async_computation.1 | async-start | bytes 1572864 | tf_op jit(solution)/shard_map/while/body/eval_jaxpr/psum | solution.py:10
  850.7 89.7 %all-reduce.2.cloned.1.call-start = ((), (), s32[]{:S(2)}) async-start(), calls=%async_computation.1 | async-start | bytes 1572864 | tf_op jit(solution)/shard_map/while/body/eval_jaxpr/psum | solution.py:10
  942.5 90.0 %all-reduce.2.cloned.1.call-start = ((), (), s32[]{:S(2)}) async-start(), calls=%async_computation.1 | async-start | bytes 1572864 | tf_op jit(solution)/shard_map/while/body/eval_jaxpr/psum | solution.py:10
  1034.6 89.7 %all-reduce.2.cloned.1.call-start = ((), (), s32[]{:S(2)}) async-start(), calls=%async_computation.1 | async-start | bytes 1572864 | tf_op jit(solution)/shard_map/while/body/eval_jaxpr/psum | solution.py:10
  1126.4 90.0 %all-reduce.2.cloned.1.call-start = ((), (), s32[]{:S(2)}) async-start(), calls=%async_computation.1 | async-start | bytes 1572864 | tf_op jit(solution)/shard_map/while/body/eval_jaxpr/psum | solution.py:10
  1218.5 89.7 %all-reduce.2.cloned.1.call-start = ((), (), s32[]{:S(2)}) async-start(), calls=%async_computation.1 | async-start | bytes 1572864 | tf_op jit(solution)/shard_map/while/body/eval_jaxpr/psum | solution.py:10
  1310.3 89.7 %all-reduce.2.cloned.1.call-start = ((), (), s32[]{:S(2)}) async-start(), calls=%async_computation.1 | async-start | bytes 1572864 | tf_op jit(solution)/shard_map/while/body/eval_jaxpr/psum | solution.py:10
  1402.1 89.7 %all-reduce.2.cloned.1.call-start = ((), (), s32[]{:S(2)}) async-start(), calls=%async_computation.1 | async-start | bytes 1572864 | tf_op jit(solution)/shard_map/while/body/eval_jaxpr/psum | solution.py:10
  1493.9 52.8 %all-gather.2.cloned.1.call-start = ((), (), s32[]{:S(2)}) async-start(), calls=%async_computation | async-start | bytes 9437184 | tf_op jit(solution)/shard_map/all_gather | solution.py:62
  1527.9 18.8 copy-start.3
  1994.6 1.0 copy-start.1
Sparse Core Ops, SparseCore 0:
  24.7 87.9 all-reduce.1
  119.5 85.3 all-reduce.1
  211.6 85.3 all-reduce.1
  303.4 85.3 all-reduce.1
  395.2 85.3 all-reduce.1
  487.0 85.3 all-reduce.1
  579.1 85.3 all-reduce.1
  671.2 85.3 all-reduce.1
  763.3 85.3 all-reduce.1
  855.1 85.3 all-reduce.1
  947.2 85.3 all-reduce.1
  1039.0 85.3 all-reduce.1
  1131.1 85.3 all-reduce.1
  1222.9 85.3 all-reduce.1
  1314.7 85.3 all-reduce.1
  1406.5 85.3 all-reduce.1
Sparse Core Ops, SparseCore 1:
  1496.1 50.6 all-gather.1
where the time goes:
time: 2010 us; the launch traced here: 2000 us
  waiting for transfers between devices  1430 us (71%)
  other arithmetic  278 us (14%)
  local copies, waits for them, and re-layouts  151 us (8%)
  matrix products  118 us (6%)
    psum x16, waiting for transfers between devices, spread(): return lax.psum(block, axis)  1430 us
    another operation x16, other arithmetic, row_update(): factor_chol = jnp.linalg.cholesky(gram_matrix)  141 us
    another operation x12, other arithmetic, row_update(): lax.linalg.triangular_solve(factor_chol, sampled, left_side=False, lower=...  118 us
    dot_general x26, matrix products, product_of(): return jnp.einsum(form, left, right, preferred_element_type=jnp.float32)  114 us
  transfers between devices with their start and end apart: 17, of which 17 were waited for; matrix products, arithmetic and copies ran while one was open for 2% of the time, Pallas kernels for 0%

commit v1 on v0

--- a/solution.py
+++ b/solution.py
@@ -7,7 +7,7 @@
 
 def spread(block, axis, holder):
     block = jnp.where(lax.axis_index(axis) == holder, block, jnp.zeros_like(block))
-    return lax.psum(block, axis)
+    return jnp.sum(lax.all_gather(block, axis), axis=0)
 
 
 def product_of(form, left, right):

time: 2010 us -> 2150 us (1.070)
  other arithmetic: 278 us -> 392 us
  waiting for transfers between devices: 1430 us -> 1490 us
    all_gather x0 -> x16, waiting for transfers between devices: none -> 1480 us  [spread(): return jnp.sum(lax.all_gather(block, axis), axis=0)]
    psum x16 -> x0, waiting for transfers between devices: 1430 us -> none  [spread(): return lax.psum(block, axis)]
    reduce_sum x0 -> x16, other arithmetic: none -> 114 us  [spread(): return jnp.sum(lax.all_gather(block, axis), axis=0)]
where the time goes in v1:
time: 2150 us
  waiting for transfers between devices  1490 us (69%)
  other arithmetic  392 us (18%)
  local copies, waits for them, and re-layouts  133 us (6%)
  matrix products  118 us (5%)
    all_gather x16, waiting for transfers between devices, spread(): return jnp.sum(lax.all_gather(block, axis), axis=0)  1480 us
    another operation x16, other arithmetic, row_update(): factor_chol = jnp.linalg.cholesky(gram_matrix)  141 us
    another operation x12, other arithmetic, row_update(): lax.linalg.triangular_solve(factor_chol, sampled, left_side=False, lower=...  118 us
    reduce_sum x16, other arithmetic, spread(): return jnp.sum(lax.all_gather(block, axis), axis=0)  114 us
    dot_general x26, matrix products, product_of(): return jnp.einsum(form, left, right, preferred_element_type=jnp.float32)  114 us
  transfers between devices with their start and end apart: 17, of which 17 were waited for; matrix products, arithmetic and copies ran while one was open for 2% of the time, Pallas kernels for 0%

profile of v1, /device:TPU:1, one launch (start us, length us, event | category | flops | bytes accessed | tf_op | source)
XLA Modules:
  0.0 2152.1 jit_solution(8135223612068258241)
XLA Ops:
  20.1 1624.2 %while.31 = (s32[]{:T(128)}, bf16[32,6,256,128]{3,2,1,0:T(8,128)(2,1)}, bf16[2,6,256,128]{3,2,1,0:T(8,128)(2,1)S(1)}, s32[]{:T(128)}, u32[]{:T(128)}, /*index=5*...) while((s32[]{:T(128)}, bf16[32,6,256,128]{3,2,1,0:T(8,128)(2,1)}, ...), condition=%wide.region_2.3_spmd, body=%wide.region_0.2_spmd.sunk | while | flops 6291466 | bytes 56623336 | solution.py:73
  21.1 96.0 %all-gather.8.cloned.1.call-done = bf16[32,6,256,128]{3,2,1,0:T(8,128)(2,1)} async-done(((bf16[2,6,256,128]{3,2,1,0:T(8,128)(2,1)}), bf16[32,6,256,128]{3,2,1,0:T(8,128)(2,1)}) %all-gather.8.cloned.1.call-update) | async-done | bytes 12582928 | tf_op jit(solution)/shard_map/while/body/eval_jaxpr/all_gather | solution.py:10
  126.2 92.4 %all-gather.8.cloned.1.call-done = bf16[32,6,256,128]{3,2,1,0:T(8,128)(2,1)} async-done(((bf16[2,6,256,128]{3,2,1,0:T(8,128)(2,1)}), bf16[32,6,256,128]{3,2,1,0:T(8,128)(2,1)}) %all-gather.8.cloned.1.call-update) | async-done | bytes 12582928 | tf_op jit(solution)/shard_map/while/body/eval_jaxpr/all_gather | solution.py:10
  227.6 92.4 %all-gather.8.cloned.1.call-done = bf16[32,6,256,128]{3,2,1,0:T(8,128)(2,1)} async-done(((bf16[2,6,256,128]{3,2,1,0:T(8,128)(2,1)}), bf16[32,6,256,128]{3,2,1,0:T(8,128)(2,1)}) %all-gather.8.cloned.1.call-update) | async-done | bytes 12582928 | tf_op jit(solution)/shard_map/while/body/eval_jaxpr/all_gather | solution.py:10
  329.0 92.1 %all-gather.8.cloned.1.call-done = bf16[32,6,256,128]{3,2,1,0:T(8,128)(2,1)} async-done(((bf16[2,6,256,128]{3,2,1,0:T(8,128)(2,1)}), bf16[32,6,256,128]{3,2,1,0:T(8,128)(2,1)}) %all-gather.8.cloned.1.call-update) | async-done | bytes 12582928 | tf_op jit(solution)/shard_map/while/body/eval_jaxpr/all_gather | solution.py:10
  430.2 92.1 %all-gather.8.cloned.1.call-done = bf16[32,6,256,128]{3,2,1,0:T(8,128)(2,1)} async-done(((bf16[2,6,256,128]{3,2,1,0:T(8,128)(2,1)}), bf16[32,6,256,128]{3,2,1,0:T(8,128)(2,1)}) %all-gather.8.cloned.1.call-update) | async-done | bytes 12582928 | tf_op jit(solution)/shard_map/while/body/eval_jaxpr/all_gather | solution.py:10
  531.3 92.1 %all-gather.8.cloned.1.call-done = bf16[32,6,256,128]{3,2,1,0:T(8,128)(2,1)} async-done(((bf16[2,6,256,128]{3,2,1,0:T(8,128)(2,1)}), bf16[32,6,256,128]{3,2,1,0:T(8,128)(2,1)}) %all-gather.8.cloned.1.call-update) | async-done | bytes 12582928 | tf_op jit(solution)/shard_map/while/body/eval_jaxpr/all_gather | solution.py:10
  632.4 92.4 %all-gather.8.cloned.1.call-done = bf16[32,6,256,128]{3,2,1,0:T(8,128)(2,1)} async-done(((bf16[2,6,256,128]{3,2,1,0:T(8,128)(2,1)}), bf16[32,6,256,128]{3,2,1,0:T(8,128)(2,1)}) %all-gather.8.cloned.1.call-update) | async-done | bytes 12582928 | tf_op jit(solution)/shard_map/while/body/eval_jaxpr/all_gather | solution.py:10
  733.9 92.4 %all-gather.8.cloned.1.call-done = bf16[32,6,256,128]{3,2,1,0:T(8,128)(2,1)} async-done(((bf16[2,6,256,128]{3,2,1,0:T(8,128)(2,1)}), bf16[32,6,256,128]{3,2,1,0:T(8,128)(2,1)}) %all-gather.8.cloned.1.call-update) | async-done | bytes 12582928 | tf_op jit(solution)/shard_map/while/body/eval_jaxpr/all_gather | solution.py:10
  835.3 92.4 %all-gather.8.cloned.1.call-done = bf16[32,6,256,128]{3,2,1,0:T(8,128)(2,1)} async-done(((bf16[2,6,256,128]{3,2,1,0:T(8,128)(2,1)}), bf16[32,6,256,128]{3,2,1,0:T(8,128)(2,1)}) %all-gather.8.cloned.1.call-update) | async-done | bytes 12582928 | tf_op jit(solution)/shard_map/while/body/eval_jaxpr/all_gather | solution.py:10
  936.7 92.1 %all-gather.8.cloned.1.call-done = bf16[32,6,256,128]{3,2,1,0:T(8,128)(2,1)} async-done(((bf16[2,6,256,128]{3,2,1,0:T(8,128)(2,1)}), bf16[32,6,256,128]{3,2,1,0:T(8,128)(2,1)}) %all-gather.8.cloned.1.call-update) | async-done | bytes 12582928 | tf_op jit(solution)/shard_map/while/body/eval_jaxpr/all_gather | solution.py:10
  1037.8 92.4 %all-gather.8.cloned.1.call-done = bf16[32,6,256,128]{3,2,1,0:T(8,128)(2,1)} async-done(((bf16[2,6,256,128]{3,2,1,0:T(8,128)(2,1)}), bf16[32,6,256,128]{3,2,1,0:T(8,128)(2,1)}) %all-gather.8.cloned.1.call-update) | async-done | bytes 12582928 | tf_op jit(solution)/shard_map/while/body/eval_jaxpr/all_gather | solution.py:10
  1139.3 92.1 %all-gather.8.cloned.1.call-done = bf16[32,6,256,128]{3,2,1,0:T(8,128)(2,1)} async-done(((bf16[2,6,256,128]{3,2,1,0:T(8,128)(2,1)}), bf16[32,6,256,128]{3,2,1,0:T(8,128)(2,1)}) %all-gather.8.cloned.1.call-update) | async-done | bytes 12582928 | tf_op jit(solution)/shard_map/while/body/eval_jaxpr/all_gather | solution.py:10
  1240.4 92.4 %all-gather.8.cloned.1.call-done = bf16[32,6,256,128]{3,2,1,0:T(8,128)(2,1)} async-done(((bf16[2,6,256,128]{3,2,1,0:T(8,128)(2,1)}), bf16[32,6,256,128]{3,2,1,0:T(8,128)(2,1)}) %all-gather.8.cloned.1.call-update) | async-done | bytes 12582928 | tf_op jit(solution)/shard_map/while/body/eval_jaxpr/all_gather | solution.py:10
  1341.9 92.1 %all-gather.8.cloned.1.call-done = bf16[32,6,256,128]{3,2,1,0:T(8,128)(2,1)} async-done(((bf16[2,6,256,128]{3,2,1,0:T(8,128)(2,1)}), bf16[32,6,256,128]{3,2,1,0:T(8,128)(2,1)}) %all-gather.8.cloned.1.call-update) | async-done | bytes 12582928 | tf_op jit(solution)/shard_map/while/body/eval_jaxpr/all_gather | solution.py:10
  1443.0 92.1 %all-gather.8.cloned.1.call-done = bf16[32,6,256,128]{3,2,1,0:T(8,128)(2,1)} async-done(((bf16[2,6,256,128]{3,2,1,0:T(8,128)(2,1)}), bf16[32,6,256,128]{3,2,1,0:T(8,128)(2,1)}) %all-gather.8.cloned.1.call-update) | async-done | bytes 12582928 | tf_op jit(solution)/shard_map/while/body/eval_jaxpr/all_gather | solution.py:10
  1544.1 92.1 %all-gather.8.cloned.1.call-done = bf16[32,6,256,128]{3,2,1,0:T(8,128)(2,1)} async-done(((bf16[2,6,256,128]{3,2,1,0:T(8,128)(2,1)}), bf16[32,6,256,128]{3,2,1,0:T(8,128)(2,1)}) %all-gather.8.cloned.1.call-update) | async-done | bytes 12582928 | tf_op jit(solution)/shard_map/while/body/eval_jaxpr/all_gather | solution.py:10
  1644.9 16.8 copy.60
  1661.6 16.6 copy.62
  1696.1 447.8 %while.32 = (s32[]{:T(128)}, bf16[4,1,256,256]{3,2,1,0:T(8,128)(2,1)}, bf16[4,6,256,128]{3,2,1,0:T(8,128)(2,1)}, bf16[4,1,256,256]{3,2,1,0:T(8,128)(2,1)}, s32[4...) while((s32[]{:T(128)}, ...), condition=%wide.region_6.7_spmd, body=%wide.region_3.6_spmd.sunk | while | flops 2490991104 | bytes 93083896 | solution.py:78
  1702.5 10.2 convolution_convert_fusion.5
  1720.8 35.2 %custom-call.15 = f32[6,64,64]{2,1,0:T(8,128)S(1)} custom-call(f32[6,64,64]{2,1,0:T(8,128)S(1)} %fusion.126), custom_call_target="Cholesky" | custom-call | tf_op jit(solution)/shard_map/while/body/eval_jaxpr/jit(cholesky)/cholesky | solution.py:40
  1756.2 29.5 %custom-call.16 = f32[6,1,64,64]{2,3,1,0:T(8,128)S(1)} custom-call(f32[6,1,64,64]{3,2,1,0:T(8,128)S(1)} %select_bitcast_fusion.2), custom_call_target="InvertDiagBlocksLowerTriangular" | custom-call | tf_op jit(solution)/shard_map/while/body/eval_jaxpr/triangular_solve | solution.py:41
  1814.5 10.2 convolution_convert_fusion.5
  1832.7 35.2 %custom-call.15 = f32[6,64,64]{2,1,0:T(8,128)S(1)} custom-call(f32[6,64,64]{2,1,0:T(8,128)S(1)} %fusion.126), custom_call_target="Cholesky" | custom-call | tf_op jit(solution)/shard_map/while/body/eval_jaxpr/jit(cholesky)/cholesky | solution.py:40
  1868.2 29.5 %custom-call.16 = f32[6,1,64,64]{2,3,1,0:T(8,128)S(1)} custom-call(f32[6,1,64,64]{3,2,1,0:T(8,128)S(1)} %select_bitcast_fusion.2), custom_call_target="InvertDiagBlocksLowerTriangular" | custom-call | tf_op jit(solution)/shard_map/while/body/eval_jaxpr/triangular_solve | solution.py:41
  1926.4 10.2 convolution_convert_fusion.5
  1944.7 35.2 %custom-call.15 = f32[6,64,64]{2,1,0:T(8,128)S(1)} custom-call(f32[6,64,64]{2,1,0:T(8,128)S(1)} %fusion.126), custom_call_target="Cholesky" | custom-call | tf_op jit(solution)/shard_map/while/body/eval_jaxpr/jit(cholesky)/cholesky | solution.py:40
  1980.1 29.5 %custom-call.16 = f32[6,1,64,64]{2,3,1,0:T(8,128)S(1)} custom-call(f32[6,1,64,64]{3,2,1,0:T(8,128)S(1)} %select_bitcast_fusion.2), custom_call_target="InvertDiagBlocksLowerTriangular" | custom-call | tf_op jit(solution)/shard_map/while/body/eval_jaxpr/triangular_solve | solution.py:41
  2038.4 10.2 convolution_convert_fusion.5
  2056.6 35.2 %custom-call.15 = f32[6,64,64]{2,1,0:T(8,128)S(1)} custom-call(f32[6,64,64]{2,1,0:T(8,128)S(1)} %fusion.126), custom_call_target="Cholesky" | custom-call | tf_op jit(solution)/shard_map/while/body/eval_jaxpr/jit(cholesky)/cholesky | solution.py:40
  2092.1 29.5 %custom-call.16 = f32[6,1,64,64]{2,3,1,0:T(8,128)S(1)} custom-call(f32[6,1,64,64]{3,2,1,0:T(8,128)S(1)} %select_bitcast_fusion.2), custom_call_target="InvertDiagBlocksLowerTriangular" | custom-call | tf_op jit(solution)/shard_map/while/body/eval_jaxpr/triangular_solve | solution.py:41
  (201 shorter events, 317.3 us)
Async XLA Ops:
  8.0 2.4 copy-start
  12.3 7.8 copy-start.2
  20.1 97.0 %all-gather.8.cloned.1.call-start = ((), (), s32[]{:S(2)}) async-start(), calls=%async_computation.1 | async-start | bytes 13369344 | tf_op jit(solution)/shard_map/while/body/eval_jaxpr/all_gather | solution.py:10
  125.2 93.3 %all-gather.8.cloned.1.call-start = ((), (), s32[]{:S(2)}) async-start(), calls=%async_computation.1 | async-start | bytes 13369344 | tf_op jit(solution)/shard_map/while/body/eval_jaxpr/all_gather | solution.py:10
  226.6 93.3 %all-gather.8.cloned.1.call-start = ((), (), s32[]{:S(2)}) async-start(), calls=%async_computation.1 | async-start | bytes 13369344 | tf_op jit(solution)/shard_map/while/body/eval_jaxpr/all_gather | solution.py:10
  328.1 93.0 %all-gather.8.cloned.1.call-start = ((), (), s32[]{:S(2)}) async-start(), calls=%async_computation.1 | async-start | bytes 13369344 | tf_op jit(solution)/shard_map/while/body/eval_jaxpr/all_gather | solution.py:10
  429.2 93.0 %all-gather.8.cloned.1.call-start = ((), (), s32[]{:S(2)}) async-start(), calls=%async_computation.1 | async-start | bytes 13369344 | tf_op jit(solution)/shard_map/while/body/eval_jaxpr/all_gather | solution.py:10
  530.3 93.0 %all-gather.8.cloned.1.call-start = ((), (), s32[]{:S(2)}) async-start(), calls=%async_computation.1 | async-start | bytes 13369344 | tf_op jit(solution)/shard_map/while/body/eval_jaxpr/all_gather | solution.py:10
  631.4 93.3 %all-gather.8.cloned.1.call-start = ((), (), s32[]{:S(2)}) async-start(), calls=%async_computation.1 | async-start | bytes 13369344 | tf_op jit(solution)/shard_map/while/body/eval_jaxpr/all_gather | solution.py:10
  732.9 93.3 %all-gather.8.cloned.1.call-start = ((), (), s32[]{:S(2)}) async-start(), calls=%async_computation.1 | async-start | bytes 13369344 | tf_op jit(solution)/shard_map/while/body/eval_jaxpr/all_gather | solution.py:10
  834.3 93.3 %all-gather.8.cloned.1.call-start = ((), (), s32[]{:S(2)}) async-start(), calls=%async_computation.1 | async-start | bytes 13369344 | tf_op jit(solution)/shard_map/while/body/eval_jaxpr/all_gather | solution.py:10
  935.7 93.0 %all-gather.8.cloned.1.call-start = ((), (), s32[]{:S(2)}) async-start(), calls=%async_computation.1 | async-start | bytes 13369344 | tf_op jit(solution)/shard_map/while/body/eval_jaxpr/all_gather | solution.py:10
  1036.9 93.3 %all-gather.8.cloned.1.call-start = ((), (), s32[]{:S(2)}) async-start(), calls=%async_computation.1 | async-start | bytes 13369344 | tf_op jit(solution)/shard_map/while/body/eval_jaxpr/all_gather | solution.py:10
  1138.3 93.0 %all-gather.8.cloned.1.call-start = ((), (), s32[]{:S(2)}) async-start(), calls=%async_computation.1 | async-start | bytes 13369344 | tf_op jit(solution)/shard_map/while/body/eval_jaxpr/all_gather | solution.py:10
  1239.4 93.3 %all-gather.8.cloned.1.call-start = ((), (), s32[]{:S(2)}) async-start(), calls=%async_computation.1 | async-start | bytes 13369344 | tf_op jit(solution)/shard_map/while/body/eval_jaxpr/all_gather | solution.py:10
  1340.9 93.0 %all-gather.8.cloned.1.call-start = ((), (), s32[]{:S(2)}) async-start(), calls=%async_computation.1 | async-start | bytes 13369344 | tf_op jit(solution)/shard_map/while/body/eval_jaxpr/all_gather | solution.py:10
  1442.0 93.0 %all-gather.8.cloned.1.call-start = ((), (), s32[]{:S(2)}) async-start(), calls=%async_computation.1 | async-start | bytes 13369344 | tf_op jit(solution)/shard_map/while/body/eval_jaxpr/all_gather | solution.py:10
  1543.1 93.0 %all-gather.8.cloned.1.call-start = ((), (), s32[]{:S(2)}) async-start(), calls=%async_computation.1 | async-start | bytes 13369344 | tf_op jit(solution)/shard_map/while/body/eval_jaxpr/all_gather | solution.py:10
  1644.3 51.8 %all-gather.6.cloned.1.call-start = ((), (), s32[]{:S(2)}) async-start(), calls=%async_computation | async-start | bytes 9437184 | tf_op jit(solution)/shard_map/all_gather | solution.py:62
  1678.2 17.9 copy-start.3
  2143.9 1.0 copy-start.1
Sparse Core Ops, SparseCore 0:
  23.7 93.3 all-gather.7
  128.8 89.7 all-gather.7
  230.2 89.7 all-gather.7
  331.3 89.7 all-gather.7
  432.5 89.7 all-gather.7
  533.6 89.7 all-gather.7
  635.0 89.7 all-gather.7
  736.5 89.7 all-gather.7
  837.9 89.7 all-gather.7
  939.0 89.7 all-gather.7
  1040.5 89.7 all-gather.7
  1141.6 89.7 all-gather.7
  1243.0 89.7 all-gather.7
  1344.2 89.7 all-gather.7
  1445.3 89.7 all-gather.7
  1546.4 89.7 all-gather.7
Sparse Core Ops, SparseCore 1:
  1646.5 49.5 all-gather.5
